TPU v7x, 32 devices: a whole 2x2x4 slice. The times are simulated.
32 devices in a mesh: expert: 4 (over y, x), dp: 8 (over z, core).
Axes of the slice: x: 2, y: 2, z: 4, core: 2. Of those that a mesh axis runs over, the one named last changes fastest.
Arguments:
- gradient: bfloat16 [4, 8, 32, 4096], P('expert', 'dp'), may hold values from -6700 to 6700
- momentum: float32 [4, 32, 4096], P('expert'), may hold values from -4 to 4
- variance: bfloat16 [4, 32, 4096], P('expert'), may hold values from 0.0099487305 to 1
- worker_error: float32 [4, 8, 32, 4096], P('expert', 'dp'), may hold values from -6 to 6
- server_error: float32 [4, 32, 4096], P('expert', 'dp'), may hold values from -4 to 4
Outputs:
- new_momentum: float32 [4, 32, 4096], P('expert')
- adam_step: bfloat16 [4, 32, 4096], P('expert')
- new_worker_error: float32 [4, 8, 32, 4096], P('expert', 'dp')
- new_server_error: float32 [4, 32, 4096], P('expert', 'dp')
All inputs are finite; a program needn't handle non-finite values. Where the computation divides by a largest or mean magnitude, that divisor is 1e-20 or more.
Results may differ from a plain program's by a relative error of at most 0.011.
Values may be sent and summed in bfloat16 or wider, within the bound.
No kernel may reach another device: no remote copies, remote signals or barrier semaphores. Data moves between devices by JAX's collectives and lax.ppermute only.
A program may use at most 128 MiB of HBM per device.

v0:
```python
import jax
import jax.numpy as jnp
from jax import lax
from jax.sharding import PartitionSpec as P

beta_one = 0.9
rms_limit = 5.0
scale_eps = 1e-06
adam_eps = 1e-08


def compress(values):
    row_scale = jnp.mean(jnp.abs(values), axis=-1, keepdims=True).astype(jnp.bfloat16)
    row_code = jnp.clip(values / (row_scale.astype(jnp.float32) + scale_eps), -1.0, 1.0).astype(
        jnp.bfloat16
    )
    decoded = row_scale.astype(jnp.float32) * row_code.astype(jnp.float32)
    return (row_scale, row_code, decoded)


def per_device(gradient, momentum, variance, worker_error, server_error):
    grad_local = gradient[0, 0].astype(jnp.float32)
    squares = lax.psum(jnp.sum(jnp.square(grad_local)), "expert")
    entry_count = lax.axis_size("expert") * grad_local.shape[0] * grad_local.shape[1]
    root_mean = jnp.sqrt(squares / entry_count + 1e-06)
    clip_factor = jnp.minimum(1.0, rms_limit / root_mean)
    clipped = grad_local * clip_factor
    compensated = beta_one * momentum[0] + (1.0 - beta_one) * clipped + worker_error[0, 0]
    row_scale, row_code, decoded = compress(compensated)
    worker_new = compensated - decoded
    replicas = lax.axis_size("dp")
    group_rows = server_error.shape[1]
    codes_in, scales_in = (
        lax.all_to_all(row_code, "dp", split_axis=0, concat_axis=0, tiled=True),
        lax.all_to_all(row_scale, "dp", split_axis=0, concat_axis=0, tiled=True),
    )
    products = scales_in.astype(jnp.float32) * codes_in.astype(jnp.float32)
    average = jnp.sum(products.reshape(replicas, group_rows, products.shape[1]), axis=0) / replicas
    combined = average + server_error[0]
    owner_scale, owner_code, owner_decoded = compress(combined)
    server_new = combined - owner_decoded
    codes_all, scales_all = (
        lax.all_gather(owner_code, "dp", axis=0, tiled=True),
        lax.all_gather(owner_scale, "dp", axis=0, tiled=True),
    )
    momentum_new = scales_all.astype(jnp.float32) * codes_all.astype(jnp.float32)
    step_out = (momentum_new / (jnp.sqrt(variance[0].astype(jnp.float32)) + adam_eps)).astype(
        jnp.bfloat16
    )
    return (momentum_new[None], step_out[None], worker_new[None, None], server_new[None])


def solution(mesh):
    placed = (
        P("expert", "dp", None, None),
        P("expert", None, None),
        P("expert", None, None),
        P("expert", "dp", None, None),
        P("expert", "dp", None),
    )
    return jax.shard_map(
        per_device,
        mesh=mesh,
        in_specs=placed,
        out_specs=(
            P("expert", None, None),
            P("expert", None, None),
            P("expert", "dp", None, None),
            P("expert", "dp", None),
        ),
        check_vma=False,
    )
```

profile of v0, /device:TPU:0, one launch (start us, length us, event | category | flops | bytes accessed | tf_op | source)
XLA Modules:
  0.0 72.4 jit_solution(1911349935368470256)
XLA Ops:
  0.6 0.0 copy-start.2
  0.6 1.8 %fusion = f32[]{:T(128)} fusion(bf16[1,1,32,4096]{3,2,1,0:T(8,128)(2,1)} %param.5), kind=kLoop, calls=%fused_computation.2 | loop fusion | flops 393215 | bytes 262148 | tf_op jit(solution)/shard_map/reduce_sum | solution.py:23
  2.4 12.0 %psum.7 = f32[]{:T(128)} all-reduce(f32[]{:T(128)} %fusion), channel_id=1, replica_groups=mesh['expert'=4,'dp'=8] {'expert'}, use_global_device_ids=true, to_apply=%region_1.0 | all-reduce | flops 1 | bytes 8 | tf_op jit(solution)/shard_map/psum | solution.py:23
  15.1 0.0 copy-done.2
  15.1 0.0 copy-start.1
  15.1 1.5 %fusion.5 = f32[32]{0:T(128)S(1)} fusion(f32[1,1,32,4096]{3,2,1,0:T(8,128)} %param.8, f32[]{:T(128)S(6)} %min.27, bf16[1,1,32,4096]{3,2,1,0:T(8,128)(2,1)S(1)} %copy-done.2, f32[1,32,4096]{2,1,0:T(8,128)} %param.6), kind=kLoop, calls=%fused_computation.10 | loop fusion | flops 1048544 | bytes 1310852 | tf_op jit(solution)/shard_map/reduce_sum | solution.py:13
  16.6 0.7 convert_element_type.145
  17.3 4.9 %all-to-all-start = ((bf16[8,4,1]{1,2,0:T(2,128)(2,1)}), bf16[8,4,1]{1,2,0:T(2,128)(2,1)S(1)}, u32[]{:S(2)}, u32[]{:S(2)}) async-start(bf16[8,4,1]{1,2,0:T(2,128)(2,1)} %convert_element_type.145), calls=%async_computation | async-start | bytes 8192 | tf_op jit(solution)/shard_map/all_to_all | solution.py:35
  22.2 0.0 copy-done.1
  22.2 0.0 copy-start
  22.3 1.0 %copy-done = f32[1,1,32,4096]{3,2,1,0:T(8,128)S(1)} copy-done((f32[1,1,32,4096]{3,2,1,0:T(8,128)S(1)}, f32[1,1,32,4096]{3,2,1,0:T(8,128)}, u32[]{:S(2)}) %copy-start) | copy-done | bytes 524312
  23.2 0.1 squeeze.12
  23.4 0.1 add.68
  23.5 1.0 %multiply_subtract_fusion = (f32[1,1,32,4096]{3,2,1,0:T(8,128)}, f32[1,1,32,4096]{3,2,1,0:T(8,128)S(1)}) fusion(f32[1,1,32,4096]{3,2,1,0:T(8,128)S(1)} %copy-done, f32[32]{0:T(128)S(1)} %get-tuple-element.12, f32[32]{0:T(128)S(1)} %get-tuple-element.11, f32[]{:T(128)S(6)} %min.27, bf16[1,1,32,4096]{3,2,1,0:T(8,128)(2,1)S(1)} %copy-done.2, ...), kind=kLoop, calls=%fused_computation.12 | loop fusion | flops 1572864 | bytes 2359556 | tf_op jit(solution)/shard_map/sub | solution.py:30
  24.4 0.1 mul.97
  24.6 0.1 mul.96
  24.7 1.0 %clamp_convert_fusion.1 = bf16[8,4,4096]{2,1,0:T(4,128)(2,1)} fusion(f32[8,4,4096]{2,1,0:T(4,128)S(1)} %squeeze.12, f32[8,4,4096]{2,1,0:T(4,128)S(1)} %mul.96, f32[8,4,4096]{2,1,0:T(4,128)S(1)} %mul.97, f32[8,4]{1,0:T(8,128)S(1)} %add.68), kind=kLoop, calls=%fused_computation.15 | loop fusion | flops 655360 | bytes 1835136 | tf_op jit(solution)/shard_map/convert_element_type | solution.py:14
  25.7 2.0 %all-to-all-done = bf16[8,4,1]{1,2,0:T(2,128)(2,1)S(1)} async-done(((bf16[8,4,1]{1,2,0:T(2,128)(2,1)}), bf16[8,4,1]{1,2,0:T(2,128)(2,1)S(1)}, u32[]{:S(2)}, u32[]{:S(2)}) %all-to-all-start) | async-done | bytes 96 | tf_op jit(solution)/shard_map/all_to_all | solution.py:35
  27.7 3.4 %all-to-all-start.1 = ((bf16[8,4,4096]{2,1,0:T(4,128)(2,1)}), bf16[8,4,4096]{2,1,0:T(4,128)(2,1)S(1)}, u32[]{:S(2)}, u32[]{:S(2)}) async-start(bf16[8,4,4096]{2,1,0:T(4,128)(2,1)} %clamp_convert_fusion.1), calls=%async_computation.1 | async-start | bytes 524288 | tf_op jit(solution)/shard_map/all_to_all | solution.py:34
  31.1 0.0 copy-start.5
  31.1 0.6 copy-done.5
  31.8 0.6 dynamic-slice
  33.0 0.1 copy.17
  33.1 0.1 copy.18
  33.2 0.0 copy-start.3
  33.2 7.5 %all-to-all-done.1 = bf16[8,4,4096]{2,1,0:T(4,128)(2,1)S(1)} async-done(((bf16[8,4,4096]{2,1,0:T(4,128)(2,1)}), bf16[8,4,4096]{2,1,0:T(4,128)(2,1)S(1)}, u32[]{:S(2)}, u32[]{:S(2)}) %all-to-all-start.1) | async-done | bytes 262176 | tf_op jit(solution)/shard_map/all_to_all | solution.py:34
  40.8 0.2 multiply_reduce_fusion
  41.0 0.0 copy-done.3
  41.0 0.1 abs_reduce_fusion
  41.1 0.1 fusion.7
  41.2 14.2 %all-gather.1 = bf16[8,4,4096]{2,1,0:T(4,128)(2,1)S(1)} all-gather(bf16[1,4,4096]{2,1,0:T(4,128)(2,1)S(1)} %fusion.7), channel_id=1, replica_groups=mesh['expert'=4,'dp'=8] {'dp'}, dimensions={0}, use_global_device_ids=true | all-gather | bytes 294912 | tf_op jit(solution)/shard_map/all_gather | solution.py:43
  55.4 0.0 copy-start.4
  55.5 0.2 dynamic-update-slice
  55.7 14.8 %all-reduce = bf16[32]{0:T(256)(128)(2,1)S(1)} all-reduce(bf16[32]{0:T(256)(128)(2,1)S(1)} %dynamic-update-slice), channel_id=2, replica_groups=mesh['expert'=4,'dp'=8] {'dp'}, use_global_device_ids=true, to_apply=%add | all-reduce | flops 32 | bytes 128
  70.6 0.7 multiply_subtract_fusion.1
  71.3 0.0 copy-done.4
  71.3 1.1 %fusion.6 = (bf16[1,32,4096]{2,1,0:T(8,128)(2,1)}, f32[1,32,4096]{2,1,0:T(8,128)}) fusion(bf16[1,32,4096]{2,1,0:T(8,128)(2,1)S(1)} %copy-done.4, f32[32,4096]{1,0:T(8,128)S(1)} %reshape.172, f32[32]{0:T(128)S(1)} %mul.109), kind=kLoop, calls=%fused_computation.18 | loop fusion | flops 655360 | bytes 1572992 | tf_op jit(solution)/shard_map/broadcast_in_dim | solution.py:50
  (7 shorter events, 0.1 us)
Async XLA Ops:
  0.6 14.4 %copy-start.2 = (bf16[1,1,32,4096]{3,2,1,0:T(8,128)(2,1)S(1)}, bf16[1,1,32,4096]{3,2,1,0:T(8,128)(2,1)}, u32[]{:S(2)}) copy-start(bf16[1,1,32,4096]{3,2,1,0:T(8,128)(2,1)} %param.5) | copy-start | bytes 786436
  15.1 7.1 %copy-start.1 = (f32[1,32,4096]{2,1,0:T(8,128)S(1)}, f32[1,32,4096]{2,1,0:T(8,128)}, u32[]{:S(2)}) copy-start(f32[1,32,4096]{2,1,0:T(8,128)} %param.6) | copy-start | bytes 1572868
  17.3 10.4 %all-to-all-start = ((bf16[8,4,1]{1,2,0:T(2,128)(2,1)}), bf16[8,4,1]{1,2,0:T(2,128)(2,1)S(1)}, u32[]{:S(2)}, u32[]{:S(2)}) async-start(bf16[8,4,1]{1,2,0:T(2,128)(2,1)} %convert_element_type.145), calls=%async_computation | async-start | bytes 8192 | tf_op jit(solution)/shard_map/all_to_all | solution.py:35
  22.2 1.0 %copy-start = (f32[1,1,32,4096]{3,2,1,0:T(8,128)S(1)}, f32[1,1,32,4096]{3,2,1,0:T(8,128)}, u32[]{:S(2)}) copy-start(f32[1,1,32,4096]{3,2,1,0:T(8,128)} %param.8) | copy-start | bytes 1572868
  27.7 13.1 %all-to-all-start.1 = ((bf16[8,4,4096]{2,1,0:T(4,128)(2,1)}), bf16[8,4,4096]{2,1,0:T(4,128)(2,1)S(1)}, u32[]{:S(2)}, u32[]{:S(2)}) async-start(bf16[8,4,4096]{2,1,0:T(4,128)(2,1)} %clamp_convert_fusion.1), calls=%async_computation.1 | async-start | bytes 524288 | tf_op jit(solution)/shard_map/all_to_all | solution.py:34
  31.1 0.7 copy-start.5
  33.2 7.8 %copy-start.3 = (f32[1,4,4096]{2,1,0:T(4,128)S(1)}, f32[1,4,4096]{2,1,0:T(4,128)}, u32[]{:S(2)}) copy-start(f32[1,4,4096]{2,1,0:T(4,128)} %param.9) | copy-start | bytes 196612
  55.4 15.8 %copy-start.4 = (bf16[1,32,4096]{2,1,0:T(8,128)(2,1)S(1)}, bf16[1,32,4096]{2,1,0:T(8,128)(2,1)}, u32[]{:S(2)}) copy-start(bf16[1,32,4096]{2,1,0:T(8,128)(2,1)} %param.7) | copy-start | bytes 786436
where the time goes:
time: 72.8 us; the launch traced here: 72.4 us
  blocking collectives  41 us (56%)
  waiting for transfers between devices  9.54 us (13%)
  starting transfers between devices  8.29 us (11%)
  other arithmetic  7.52 us (10%)
  local copies, waits for them, and re-layouts  3.91 us (5%)
  between operations  2.09 us (3%)
    unnamed x1, blocking collectives  14.8 us
    all_gather x1, blocking collectives, per_device(): lax.all_gather(owner_code, 'dp', axis=0, tiled=True)  14.2 us
    psum x1, blocking collectives, per_device(): squares = lax.psum(jnp.sum(jnp.square(grad_local)), 'expert')  12 us
    all_to_all x1, waiting for transfers between devices, per_device(): lax.all_to_all(row_code, 'dp', split_axis=0, concat_axis=0, tiled=True)  7.55 us
    all_to_all x1, starting transfers between devices, per_device(): lax.all_to_all(row_scale, 'dp', split_axis=0, concat_axis=0, tiled=True)  4.88 us
    all_to_all x1, starting transfers between devices, per_device(): lax.all_to_all(row_code, 'dp', split_axis=0, concat_axis=0, tiled=True)  3.41 us
    unnamed x15, local copies, waits for them, and re-layouts  2.48 us
    all_to_all x1, waiting for transfers between devices, per_device(): lax.all_to_all(row_scale, 'dp', split_axis=0, concat_axis=0, tiled=True)  1.99 us
  transfers between devices with their start and end apart: 2, of which 2 were waited for; matrix products, arithmetic and copies ran while one was open for 5% of the time, Pallas kernels for 0%

commit v1 on v0

--- a/solution.py
+++ b/solution.py
@@ -7,6 +7,27 @@
 rms_limit = 5.0
 scale_eps = 1e-06
 adam_eps = 1e-08
+
+
+def joined_along(pieces, dim):
+    pieces = jnp.moveaxis(pieces, 0, dim)
+    lengths = pieces.shape
+    return pieces.reshape(*lengths[:dim], lengths[dim] * lengths[dim + 1], *lengths[dim + 2 :])
+
+
+def grow_blocks(shard, axis):
+    size, mine = (lax.axis_size(axis), lax.axis_index(axis))
+    blocks, distance = (shard[None], 1)
+    while distance < size:
+        other = lax.ppermute(blocks, axis, [(i, i ^ distance) for i in range(size)])
+        low = mine & distance == 0
+        blocks = jnp.concatenate([jnp.where(low, blocks, other), jnp.where(low, other, blocks)])
+        distance *= 2
+    return blocks
+
+
+def doubled_up(array, axis, dim):
+    return joined_along(grow_blocks(array, axis), dim)
 
 
 def compress(values):
@@ -40,7 +61,7 @@
     owner_scale, owner_code, owner_decoded = compress(combined)
     server_new = combined - owner_decoded
     codes_all, scales_all = (
-        lax.all_gather(owner_code, "dp", axis=0, tiled=True),
+        doubled_up(owner_code, "dp", 0),
         lax.all_gather(owner_scale, "dp", axis=0, tiled=True),
     )
     momentum_new = scales_all.astype(jnp.float32) * codes_all.astype(jnp.float32)

time: 72.8 us -> 67.7 us (0.930)
  blocking collectives: 41 us -> 26.9 us
  waiting for transfers between devices: 9.54 us -> 16.8 us
  local copies, waits for them, and re-layouts: 3.91 us -> 4.8 us
    all_gather x1 -> x0, blocking collectives: 14.2 us -> none  [per_device(): lax.all_gather(owner_code, 'dp', axis=0, tiled=True)]
    ppermute x0 -> x3, waiting for transfers between devices: none -> 5.4 us  [grow_blocks(): other = lax.ppermute(blocks, axis, [(i, i ^ distance) for i in range(size)])]
    all_to_all x1, waiting for transfers between devices: 7.55 us -> 9.44 us  [per_device(): lax.all_to_all(row_code, 'dp', split_axis=0, concat_axis=0, tiled=True)]
    convert_element_type x0 -> x3, other arithmetic: none -> 1.25 us  [the longest x1 1.08 us: per_device(): (momentum_new / (jnp.sqrt(variance[0].astype(jnp.float32)) + adam_eps)).a...]
    broadcast_in_dim x1 -> x0, other arithmetic: 1.09 us -> none  [per_device(): step_out[None]]
    unnamed x15, local copies, waits for them, and re-layouts: 2.48 us -> 3.23 us
  transfers between devices with their start and end apart: 2 -> 5, of which waited for: 2 -> 4; matrix products, arithmetic and copies ran while one was open for 5% -> 5% of each run, Pallas kernels for 0% -> 0%
where the time goes in v1:
time: 67.7 us; the launch traced here: 67.2 us
  blocking collectives  26.9 us (40%)
  waiting for transfers between devices  16.8 us (25%)
  starting transfers between devices  8.51 us (13%)
  other arithmetic  8 us (12%)
  local copies, waits for them, and re-layouts  4.8 us (7%)
  between operations  2.14 us (3%)
    unnamed x1, blocking collectives  14.9 us
    psum x1, blocking collectives, per_device(): squares = lax.psum(jnp.sum(jnp.square(grad_local)), 'expert')  12 us
    all_to_all x1, waiting for transfers between devices, per_device(): lax.all_to_all(row_code, 'dp', split_axis=0, concat_axis=0, tiled=True)  9.44 us
    ppermute x3, waiting for transfers between devices, grow_blocks(): other = lax.ppermute(blocks, axis, [(i, i ^ distance) for i in range(size)])  5.4 us
    all_to_all x1, starting transfers between devices, per_device(): lax.all_to_all(row_scale, 'dp', split_axis=0, concat_axis=0, tiled=True)  4.88 us
    all_to_all x1, starting transfers between devices, per_device(): lax.all_to_all(row_code, 'dp', split_axis=0, concat_axis=0, tiled=True)  3.41 us
    unnamed x15, local copies, waits for them, and re-layouts  3.23 us
    all_to_all x1, waiting for transfers between devices, per_device(): lax.all_to_all(row_scale, 'dp', split_axis=0, concat_axis=0, tiled=True)  1.99 us
  transfers between devices with their start and end apart: 5, of which 4 were waited for; matrix products, arithmetic and copies ran while one was open for 5% of the time, Pallas kernels for 0%

profile of v1, /device:TPU:0, one launch (start us, length us, event | category | flops | bytes accessed | tf_op | source)
XLA Modules:
  0.0 67.2 jit_solution(12784725359980112923)
XLA Ops:
  0.6 0.0 copy-start.2
  0.6 1.8 %fusion = f32[]{:T(128)} fusion(bf16[1,1,32,4096]{3,2,1,0:T(8,128)(2,1)} %param.5), kind=kLoop, calls=%fused_computation.2 | loop fusion | flops 393215 | bytes 262148 | tf_op jit(solution)/shard_map/reduce_sum | solution.py:44
  2.4 12.0 %psum.7 = f32[]{:T(128)} all-reduce(f32[]{:T(128)} %fusion), channel_id=1, replica_groups=mesh['expert'=4,'dp'=8] {'expert'}, use_global_device_ids=true, to_apply=%region_1.0 | all-reduce | flops 1 | bytes 8 | tf_op jit(solution)/shard_map/psum | solution.py:44
  15.1 0.0 copy-done.2
  15.1 0.0 copy-start.1
  15.1 1.5 %fusion.4 = f32[32]{0:T(128)S(1)} fusion(f32[1,1,32,4096]{3,2,1,0:T(8,128)} %param.8, f32[]{:T(128)S(6)} %min.23, bf16[1,1,32,4096]{3,2,1,0:T(8,128)(2,1)S(1)} %copy-done.2, f32[1,32,4096]{2,1,0:T(8,128)} %param.6), kind=kLoop, calls=%fused_computation.8 | loop fusion | flops 1048544 | bytes 1310852 | tf_op jit(solution)/shard_map/reduce_sum | solution.py:34
  16.6 0.7 %convert_element_type.156 = bf16[8,4,1]{1,2,0:T(2,128)(2,1)} reshape(bf16[32]{0:T(256)(128)(2,1)S(1)} %get-tuple-element.18) | data formatting | bytes 128 | tf_op jit(solution)/shard_map/convert_element_type | solution.py:34
  17.3 4.9 %all-to-all-start = ((bf16[8,4,1]{1,2,0:T(2,128)(2,1)}), bf16[8,4,1]{1,2,0:T(2,128)(2,1)S(1)}, u32[]{:S(2)}, u32[]{:S(2)}) async-start(bf16[8,4,1]{1,2,0:T(2,128)(2,1)} %convert_element_type.156), calls=%async_computation | async-start | bytes 8192 | tf_op jit(solution)/shard_map/all_to_all | solution.py:56
  22.2 0.0 copy-done.1
  22.2 0.0 copy-start
  22.3 1.0 %copy-done = f32[1,1,32,4096]{3,2,1,0:T(8,128)S(1)} copy-done((f32[1,1,32,4096]{3,2,1,0:T(8,128)S(1)}, f32[1,1,32,4096]{3,2,1,0:T(8,128)}, u32[]{:S(2)}) %copy-start) | copy-done | bytes 524312
  23.2 0.1 squeeze.12
  23.4 0.1 add.67
  23.5 1.0 %multiply_subtract_fusion = (f32[1,1,32,4096]{3,2,1,0:T(8,128)}, f32[1,1,32,4096]{3,2,1,0:T(8,128)S(1)}) fusion(f32[1,1,32,4096]{3,2,1,0:T(8,128)S(1)} %copy-done, f32[32]{0:T(128)S(1)} %get-tuple-element.17, f32[32]{0:T(128)S(1)} %get-tuple-element.16, f32[]{:T(128)S(6)} %min.23, bf16[1,1,32,4096]{3,2,1,0:T(8,128)(2,1)S(1)} %copy-done.2, ...), kind=kLoop, calls=%fused_computation.10 | loop fusion | flops 1572864 | bytes 2359556 | tf_op jit(solution)/shard_map/sub | solution.py:51
  24.4 0.1 mul.104
  24.6 0.1 mul.103
  24.7 1.0 %clamp_convert_fusion.1 = bf16[8,4,4096]{2,1,0:T(4,128)(2,1)} fusion(f32[8,4,4096]{2,1,0:T(4,128)S(1)} %squeeze.12, f32[8,4,4096]{2,1,0:T(4,128)S(1)} %mul.103, f32[8,4,4096]{2,1,0:T(4,128)S(1)} %mul.104, f32[8,4]{1,0:T(8,128)S(1)} %add.67), kind=kLoop, calls=%fused_computation.14 | loop fusion | flops 655360 | bytes 1835136 | tf_op jit(solution)/shard_map/convert_element_type | solution.py:35
  25.7 2.0 %all-to-all-done = bf16[8,4,1]{1,2,0:T(2,128)(2,1)S(1)} async-done(((bf16[8,4,1]{1,2,0:T(2,128)(2,1)}), bf16[8,4,1]{1,2,0:T(2,128)(2,1)S(1)}, u32[]{:S(2)}, u32[]{:S(2)}) %all-to-all-start) | async-done | bytes 96 | tf_op jit(solution)/shard_map/all_to_all | solution.py:56
  27.7 3.4 %all-to-all-start.1 = ((bf16[8,4,4096]{2,1,0:T(4,128)(2,1)}), bf16[8,4,4096]{2,1,0:T(4,128)(2,1)S(1)}, u32[]{:S(2)}, u32[]{:S(2)}) async-start(bf16[8,4,4096]{2,1,0:T(4,128)(2,1)} %clamp_convert_fusion.1), calls=%async_computation.1 | async-start | bytes 524288 | tf_op jit(solution)/shard_map/all_to_all | solution.py:55
  31.1 0.1 copy.17
  31.2 0.1 copy.18
  31.3 0.0 copy-start.3
  31.3 9.4 %all-to-all-done.1 = bf16[8,4,4096]{2,1,0:T(4,128)(2,1)S(1)} async-done(((bf16[8,4,4096]{2,1,0:T(4,128)(2,1)}), bf16[8,4,4096]{2,1,0:T(4,128)(2,1)S(1)}, u32[]{:S(2)}, u32[]{:S(2)}) %all-to-all-start.1) | async-done | bytes 262176 | tf_op jit(solution)/shard_map/all_to_all | solution.py:55
  40.8 0.2 multiply_reduce_fusion
  41.0 0.0 copy-done.3
  41.0 0.1 fusion.6
  41.1 0.7 %multiply_subtract_fusion.1 = (f32[1,4,4096]{2,1,0:T(4,128)}, bf16[1,4,4096]{2,1,0:T(4,128)(2,1)S(1)}) fusion(f32[4]{0:T(128)S(1)} %get-tuple-element.20, f32[1,4,4096]{2,1,0:T(4,128)S(1)} %copy-done.3, f32[4,4096]{1,0:T(4,128)S(1)} %multiply_reduce_fusion, f32[4]{0:T(128)S(1)} %get-tuple-element.21), kind=kLoop, calls=%fused_computation.26 | loop fusion | flops 131072 | bytes 229408 | tf_op jit(solution)/shard_map/sub | solution.py:62
  41.9 0.0 collective-permute-start
  41.9 1.2 %collective-permute-done = bf16[1,4,4096]{2,1,0:T(4,128)(2,1)S(1)} collective-permute-done((bf16[1,4,4096]{2,1,0:T(4,128)(2,1)S(1)}, bf16[1,4,4096]{2,1,0:T(4,128)(2,1)S(1)}, u32[]{:S(2)}, u32[]{:S(2)}) %collective-permute-start) | collective-permute-done | bytes 32800 | tf_op jit(solution)/shard_map/ppermute | solution.py:22
  43.2 0.1 collective-permute-start.1
  43.3 4.2 %collective-permute-done.1 = bf16[2,4,4096]{2,1,0:T(4,128)(2,1)S(1)} collective-permute-done((bf16[2,4,4096]{2,1,0:T(4,128)(2,1)S(1)}, bf16[2,4,4096]{2,1,0:T(4,128)(2,1)S(1)}, u32[]{:S(2)}, u32[]{:S(2)}) %collective-permute-start.1) | collective-permute-done | bytes 65568 | tf_op jit(solution)/shard_map/ppermute | solution.py:22
  47.5 0.1 broadcast_select_fusion.3
  47.6 0.1 pad_maximum_fusion
  47.7 0.1 collective-permute-start.2
  47.7 0.0 copy-start.5
  47.8 0.6 copy-done.5
  48.4 0.6 dynamic-slice
  49.7 0.2 dynamic-update-slice
  49.9 14.9 %all-reduce = bf16[32]{0:T(256)(128)(2,1)S(1)} all-reduce(bf16[32]{0:T(256)(128)(2,1)S(1)} %dynamic-update-slice), channel_id=2, replica_groups=mesh['expert'=4,'dp'=8] {'dp'}, use_global_device_ids=true, to_apply=%add | all-reduce | flops 32 | bytes 128
  64.8 0.0 collective-permute-done.2
  64.8 0.1 broadcast_select_fusion.1
  65.0 0.2 maximum_convert_fusion
  65.2 0.0 copy-start.4
  65.2 0.2 reshape.221
  65.4 0.8 %copy-done.4 = bf16[1,32,4096]{2,1,0:T(8,128)(2,1)S(1)} copy-done((bf16[1,32,4096]{2,1,0:T(8,128)(2,1)S(1)}, bf16[1,32,4096]{2,1,0:T(8,128)(2,1)}, u32[]{:S(2)}) %copy-start.4) | copy-done | bytes 262168
  66.1 1.1 %divide_convert_fusion = (bf16[1,32,4096]{2,1,0:T(8,128)(2,1)}, f32[1,32,4096]{2,1,0:T(8,128)}) fusion(bf16[1,32,4096]{2,1,0:T(8,128)(2,1)S(1)} %copy-done.4, f32[1,32,4096]{2,1,0:T(8,128)S(1)} %reshape.221, f32[32]{0:T(128)S(1)} %mul.116), kind=kLoop, calls=%fused_computation.12 | loop fusion | flops 655360 | bytes 1572992 | tf_op jit(solution)/shard_map/convert_element_type | solution.py:68
  (8 shorter events, 0.2 us)
Async XLA Ops:
  0.6 14.4 %copy-start.2 = (bf16[1,1,32,4096]{3,2,1,0:T(8,128)(2,1)S(1)}, bf16[1,1,32,4096]{3,2,1,0:T(8,128)(2,1)}, u32[]{:S(2)}) copy-start(bf16[1,1,32,4096]{3,2,1,0:T(8,128)(2,1)} %param.5) | copy-start | bytes 786436
  15.1 7.1 %copy-start.1 = (f32[1,32,4096]{2,1,0:T(8,128)S(1)}, f32[1,32,4096]{2,1,0:T(8,128)}, u32[]{:S(2)}) copy-start(f32[1,32,4096]{2,1,0:T(8,128)} %param.6) | copy-start | bytes 1572868
  17.3 10.4 %all-to-all-start = ((bf16[8,4,1]{1,2,0:T(2,128)(2,1)}), bf16[8,4,1]{1,2,0:T(2,128)(2,1)S(1)}, u32[]{:S(2)}, u32[]{:S(2)}) async-start(bf16[8,4,1]{1,2,0:T(2,128)(2,1)} %convert_element_type.156), calls=%async_computation | async-start | bytes 8192 | tf_op jit(solution)/shard_map/all_to_all | solution.py:56
  22.2 1.0 %copy-start = (f32[1,1,32,4096]{3,2,1,0:T(8,128)S(1)}, f32[1,1,32,4096]{3,2,1,0:T(8,128)}, u32[]{:S(2)}) copy-start(f32[1,1,32,4096]{3,2,1,0:T(8,128)} %param.8) | copy-start | bytes 1572868
  27.7 13.1 %all-to-all-start.1 = ((bf16[8,4,4096]{2,1,0:T(4,128)(2,1)}), bf16[8,4,4096]{2,1,0:T(4,128)(2,1)S(1)}, u32[]{:S(2)}, u32[]{:S(2)}) async-start(bf16[8,4,4096]{2,1,0:T(4,128)(2,1)} %clamp_convert_fusion.1), calls=%async_computation.1 | async-start | bytes 524288 | tf_op jit(solution)/shard_map/all_to_all | solution.py:55
  31.3 9.7 %copy-start.3 = (f32[1,4,4096]{2,1,0:T(4,128)S(1)}, f32[1,4,4096]{2,1,0:T(4,128)}, u32[]{:S(2)}) copy-start(f32[1,4,4096]{2,1,0:T(4,128)} %param.9) | copy-start | bytes 196612
  41.9 1.2 %collective-permute-start = (bf16[1,4,4096]{2,1,0:T(4,128)(2,1)S(1)}, bf16[1,4,4096]{2,1,0:T(4,128)(2,1)S(1)}, u32[]{:S(2)}, u32[]{:S(2)}) collective-permute-start(bf16[1,4,4096]{2,1,0:T(4,128)(2,1)S(1)} %get-tuple-element.5), channel_id=1, source_target_pairs={{0,1},{1,0},{2,3},{3,2},{4,5},{5,4},{6,7},{7,6},{8,9},{9,8},{10,11... | collective-permute-start | bytes 98312 | tf_op jit(solution)/shard_map/ppermute | solution.py:22
  43.2 4.3 %collective-permute-start.1 = (bf16[2,4,4096]{2,1,0:T(4,128)(2,1)S(1)}, bf16[2,4,4096]{2,1,0:T(4,128)(2,1)S(1)}, u32[]{:S(2)}, u32[]{:S(2)}) collective-permute-start(bf16[2,4,4096]{2,1,0:T(4,128)(2,1)S(1)} %pad_maximum_fusion.1), channel_id=1, source_target_pairs={{0,2},{1,3},{2,0},{3,1},{4,6},{5,7},{6,4},{7,5},{8,10},{9,11},{10,... | collective-permute-start | bytes 196616 | tf_op jit(solution)/shard_map/ppermute | solution.py:22
  47.7 17.2 %collective-permute-start.2 = (bf16[4,4,4096]{2,1,0:T(4,128)(2,1)S(1)}, bf16[4,4,4096]{2,1,0:T(4,128)(2,1)S(1)}, u32[]{:S(2)}, u32[]{:S(2)}) collective-permute-start(bf16[4,4,4096]{2,1,0:T(4,128)(2,1)S(1)} %pad_maximum_fusion), channel_id=1, source_target_pairs={{0,4},{1,5},{2,6},{3,7},{4,0},{5,1},{6,2},{7,3},{8,12},{9,13},{10,... | collective-permute-start | bytes 393224 | tf_op jit(solution)/shard_map/ppermute | solution.py:22
  47.7 0.7 copy-start.5
  65.2 1.0 %copy-start.4 = (bf16[1,32,4096]{2,1,0:T(8,128)(2,1)S(1)}, bf16[1,32,4096]{2,1,0:T(8,128)(2,1)}, u32[]{:S(2)}) copy-start(bf16[1,32,4096]{2,1,0:T(8,128)(2,1)} %param.7) | copy-start | bytes 786436
